TPU v7x, 32 devices: a whole 2x2x4 slice. The times are simulated.
32 devices in a mesh: grp: 2 (over core), dp: 4 (over y, x), sp: 4 (over z).
Axes of the slice: x: 2, y: 2, z: 4, core: 2. Of those that a mesh axis runs over, the one named last changes fastest.
Arguments:
- vis: bfloat16 [512, 5120], P(('grp', 'dp', 'sp')), may hold values from -6 to 6
- merge_weight: bfloat16 [5120, 8192], P('dp', ('grp', 'sp')), may hold values from -0.078125 to 0.078125
- img_counts: int32 [32], P('dp'), may hold values from 1 to 16
- img_pos: int32 [512], P(('grp', 'dp', 'sp')), may hold values from 0 to 127, as said below
- text: bfloat16 [4096, 8192], P(('grp', 'dp', 'sp')), may hold values from -6 to 6
- cot: bfloat16 [4096, 8192], P(('grp', 'dp', 'sp')), may hold values from -6 to 6
- gain: float32 [8192], replicated, may hold values from 0.25 to 1.75
Outputs:
- vis_grad: bfloat16 [512, 5120], P(('grp', 'dp', 'sp'))
- gain_grad: float32 [8192], replicated
Inputs may be any that keep to these rules, and one draw needn't show every extreme that they name: `img_pos`: within one device's block the 16 positions are distinct. `img_counts`: the counts of one image group sum to at most 128.
All inputs are finite; a program needn't handle non-finite values.
Results may differ from a plain program's by a relative error of at most 0.014.
Values may be sent and summed in bfloat16 or wider, within the bound.
No kernel may reach another device: no remote copies, remote signals or barrier semaphores. Data moves between devices by JAX's collectives and lax.ppermute only.
A program may use at most 128 MiB of HBM per device.

v0:
```python
import jax
import jax.numpy as jnp
from jax import lax
from jax.sharding import PartitionSpec as P


def body(vis, merge_weight, img_counts, img_pos, text, cot, gain):
    rows_dev = vis.shape[0]
    tok_rows = text.shape[0]
    group_vis = lax.all_gather(vis, ("grp", "sp"), axis=0, tiled=True)
    full_weight = lax.all_gather(merge_weight, "dp", axis=0, tiled=True)
    partial_value = jnp.dot(group_vis, full_weight, preferred_element_type=jnp.float32)
    emb = lax.all_to_all(
        partial_value.astype(jnp.bfloat16), ("grp", "sp"), split_axis=0, concat_axis=1, tiled=True
    )
    total_live = jnp.sum(img_counts)
    member = lax.axis_index("grp") * lax.axis_size("sp") + lax.axis_index("sp")
    group_row = member * rows_dev + jnp.arange(rows_dev, dtype=jnp.int32)
    live = group_row < total_live
    places = jnp.arange(tok_rows, dtype=jnp.int32)
    select = (img_pos[None, :] == places[:, None]) & live[None, :]
    taken = jnp.any(select, axis=1)
    select_b = select.astype(jnp.bfloat16)
    placed = jnp.dot(select_b, emb, preferred_element_type=jnp.float32)
    hidden = jnp.where(taken[:, None], placed, text.astype(jnp.float32))
    rinv = lax.rsqrt(jnp.mean(hidden * hidden, axis=1, keepdims=True) + 1e-06)
    cotf = cot.astype(jnp.float32)
    part_gain = jnp.sum(cotf * hidden * rinv, axis=0)
    scaled = cotf * gain[None, :]
    inner = jnp.mean(scaled * hidden, axis=1, keepdims=True)
    dhid = (rinv * scaled - hidden * rinv**3 * inner).astype(jnp.bfloat16)
    demb = jnp.dot(select_b.T, dhid, preferred_element_type=jnp.float32)
    demb = jnp.where(live[:, None], demb, 0.0).astype(jnp.bfloat16)
    returned = lax.all_to_all(demb, ("grp", "sp"), split_axis=1, concat_axis=0, tiled=True)
    terms = lax.dot_general(
        returned, full_weight, (((1,), (1,)), ((), ())), preferred_element_type=jnp.float32
    )
    vis_grad = lax.psum_scatter(
        terms.astype(jnp.bfloat16), ("grp", "sp"), scatter_dimension=0, tiled=True
    )
    gain_grad = lax.psum(part_gain, ("grp", "dp", "sp"))
    return (vis_grad, gain_grad)


def solution(mesh):
    return jax.shard_map(
        body,
        mesh=mesh,
        in_specs=(
            P(("grp", "dp", "sp"), None),
            P("dp", ("grp", "sp")),
            P("dp"),
            P(("grp", "dp", "sp")),
            P(("grp", "dp", "sp"), None),
            P(("grp", "dp", "sp"), None),
            P(),
        ),
        out_specs=(P(("grp", "dp", "sp"), None), P()),
        check_vma=False,
    )
```

profile of v0, /device:TPU:0, one launch (start us, length us, event | category | flops | bytes accessed | tf_op | source)
XLA Modules:
  0.0 229.6 jit_solution(17347707635758896386)
XLA Ops:
  7.2 0.0 all-gather.3.cloned.1.call-start
  7.2 0.7 all-gather.3.cloned.1.call-update
  7.9 0.0 all-gather.5.cloned.1.call-start
  7.9 0.7 all-gather.5.cloned.1.call-update
  8.7 27.1 %all-gather.3.cloned.1.call-done = bf16[128,5120]{1,0:T(8,128)(2,1)} async-done(((bf16[16,5120]{1,0:T(8,128)(2,1)}), bf16[128,5120]{1,0:T(8,128)(2,1)}) %all-gather.3.cloned.1.call-update) | async-done | bytes 1310736 | tf_op jit(solution)/shard_map/all_gather | solution.py:10
  35.7 106.3 %all-gather.5.cloned.1.call-done = bf16[5120,1024]{1,0:T(8,128)(2,1)} async-done(((bf16[1280,1024]{1,0:T(8,128)(2,1)}), bf16[5120,1024]{1,0:T(8,128)(2,1)}) %all-gather.5.cloned.1.call-update) | async-done | bytes 10485776 | tf_op jit(solution)/shard_map/all_gather | solution.py:11
  142.1 6.6 %convolution_convert_fusion.1 = bf16[128,1024]{1,0:T(8,128)(2,1)} fusion(bf16[128,5120]{1,0:T(8,128)(2,1)} %all-gather.3.cloned.1.call-done, bf16[5120,1024]{1,0:T(8,128)(2,1)} %all-gather.5.cloned.1.call-done), kind=kOutput, calls=%fused_computation.14 | convolution fusion | flops 1342308352 | bytes 12058624 | tf_op jit(solution)/shard_map/dot_general | solution.py:12
  148.7 4.7 %all-to-all-start = ((bf16[8,16,1024]{2,1,0:T(8,128)(2,1)}), bf16[8,16,1024]{2,1,0:T(8,128)(2,1)S(1)}, u32[]{:S(2)}, u32[]{:S(2)}) async-start(bf16[8,16,1024]{2,1,0:T(8,128)(2,1)} %bitcast), calls=%async_computation | async-start | bytes 524288 | tf_op jit(solution)/shard_map/all_to_all | solution.py:13
  153.4 0.0 reduce-scatter.2.cloned.1.call-start
  153.5 0.6 reduce_sum.36
  154.1 0.7 add_compare_fusion
  154.8 0.0 copy-done.3
  154.8 0.1 fusion.12
  154.9 7.9 %all-to-all-done = bf16[8,16,1024]{2,1,0:T(8,128)(2,1)S(1)} async-done(((bf16[8,16,1024]{2,1,0:T(8,128)(2,1)}), bf16[8,16,1024]{2,1,0:T(8,128)(2,1)S(1)}, u32[]{:S(2)}, u32[]{:S(2)}) %all-to-all-start) | async-done | bytes 262176 | tf_op jit(solution)/shard_map/all_to_all | solution.py:13
  162.8 0.0 slice-start
  162.8 1.0 multiply_reduce_fusion
  163.8 0.6 copy-done.1
  164.4 1.5 fusion.7
  165.9 1.1 fusion
  167.1 11.8 %all_to_all.38 = bf16[16,8,1024]{2,0,1:T(8,128)(2,1)S(1)} all-to-all(bf16[16,8,1024]{2,0,1:T(8,128)(2,1)S(1)} %bitcast.21), channel_id=1, replica_groups=mesh['grp'=2,'dp'=4,'sp'=4] {'grp','sp'}, dimensions={1} | all-to-all | bytes 524288 | tf_op jit(solution)/shard_map/all_to_all | solution.py:34
  178.9 0.0 slice-done.1
  178.9 4.6 %convolution_convert_fusion = bf16[128,5120]{1,0:T(8,128)(2,1)} fusion(bf16[128,1024]{1,0:T(8,128)(2,1)S(1)} %bitcast.19, bf16[5120,1024]{1,0:T(8,128)(2,1)S(1)} %bitcast.17), kind=kOutput, calls=%fused_computation.3 | convolution fusion | flops 1342832640 | bytes 12058624 | tf_op jit(solution)/shard_map/dot_general | solution.py:35
  183.5 0.0 reduce-scatter.2.cloned.1.call-update
  183.5 39.5 %psum.7 = f32[8192]{0:T(1024)} all-reduce(f32[8192]{0:T(1024)S(1)} %get-tuple-element.2), channel_id=1, replica_groups=mesh['grp'=2,'dp'=4,'sp'=4] {'grp','dp','sp'}, use_global_device_ids=true, to_apply=%region_6.7 | all-reduce | flops 8192 | bytes 65536 | tf_op jit(solution)/shard_map/psum | solution.py:41
  (18 shorter events, 0.1 us)
Async XLA Ops:
  7.2 28.6 %all-gather.3.cloned.1.call-start = ((), (), s32[]{:S(2)}) async-start(), calls=%async_computation.3 | async-start | bytes 1474560 | tf_op jit(solution)/shard_map/all_gather | solution.py:10
  7.9 134.2 %all-gather.5.cloned.1.call-start = ((), (), s32[]{:S(2)}) async-start(), calls=%async_computation.4 | async-start | bytes 13107200 | tf_op jit(solution)/shard_map/all_gather | solution.py:11
  8.6 144.8 %copy-start.4 = (s32[8]{0:T(128)S(1)}, s32[8]{0:T(128)}, u32[]{:S(2)}) copy-start(s32[8]{0:T(128)} %param.9) | copy-start | bytes 100
  8.7 146.1 %copy-start.3 = (s32[16]{0:T(128)S(1)}, s32[16]{0:T(128)}, u32[]{:S(2)}) copy-start(s32[16]{0:T(128)} %param.10) | copy-start | bytes 196
  8.7 154.1 %copy-start = (bf16[128,8192]{1,0:T(8,128)(2,1)S(1)}, bf16[128,8192]{1,0:T(8,128)(2,1)}, u32[]{:S(2)}) copy-start(bf16[128,8192]{1,0:T(8,128)(2,1)} %param.11) | copy-start | bytes 6291460
  148.7 15.1 %copy-start.2 = (f32[8192]{0:T(1024)S(1)}, f32[8192]{0:T(1024)}, u32[]{:S(2)}) copy-start(f32[8192]{0:T(1024)} %param.13) | copy-start | bytes 98308
  148.7 14.1 %all-to-all-start = ((bf16[8,16,1024]{2,1,0:T(8,128)(2,1)}), bf16[8,16,1024]{2,1,0:T(8,128)(2,1)S(1)}, u32[]{:S(2)}, u32[]{:S(2)}) async-start(bf16[8,16,1024]{2,1,0:T(8,128)(2,1)} %bitcast), calls=%async_computation | async-start | bytes 524288 | tf_op jit(solution)/shard_map/all_to_all | solution.py:13
  153.4 69.6 %reduce-scatter.2.cloned.1.call-start = ((), (), s32[]{:S(2)}) async-start(), calls=%async_computation.5 | async-start | bytes 1474560 | tf_op jit(solution)/shard_map/reduce_scatter | solution.py:38
  162.8 1.6 copy-start.1
  162.8 16.0 %slice-start = ((s8[10485760]{0:T(1024)(128)(4,1)}), s8[4194304]{0:T(1024)(128)(4,1)S(1)}, s32[]{:S(2)}) async-start(s8[10485760]{0:T(1024)(128)(4,1)} %bitcast.16), calls=%async_computation.6 | async-start | bytes 8388608
  164.4 14.5 %slice-start.1 = ((s8[10485760]{0:T(1024)(128)(4,1)}), s8[4194304]{0:T(1024)(128)(4,1)S(1)}, s32[]{:S(2)}) async-start(s8[10485760]{0:T(1024)(128)(4,1)} %bitcast.16), calls=%async_computation.7 | async-start | bytes 8388608
  165.9 13.0 %slice-start.2 = ((s8[10485760]{0:T(1024)(128)(4,1)}), s8[2097152]{0:T(1024)(128)(4,1)S(1)}, s32[]{:S(2)}) async-start(s8[10485760]{0:T(1024)(128)(4,1)} %bitcast.16), calls=%async_computation.8 | async-start | bytes 4194304
Sparse Core Ops, SparseCore 0:
  9.6 26.1 all-gather.2
  37.6 104.4 all-gather.4
  183.6 34.8 reduce-scatter.1
where the time goes:
time: 230 us
  waiting for transfers between devices  143 us (62%)
  blocking collectives  51.3 us (22%)
  between operations  13.9 us (6%)
  matrix products  13.4 us (6%)
  starting transfers between devices  4.85 us (2%)
  other arithmetic  2.91 us (1%)
    all_gather x1, waiting for transfers between devices, body(): full_weight = lax.all_gather(merge_weight, 'dp', axis=0, tiled=True)  106 us
    psum x1, blocking collectives, body(): gain_grad = lax.psum(part_gain, ('grp', 'dp', 'sp'))  39.5 us
    all_gather x1, waiting for transfers between devices, body(): group_vis = lax.all_gather(vis, ('grp', 'sp'), axis=0, tiled=True)  27.1 us
    all_to_all x1, blocking collectives, body(): lax.all_to_all(demb, ('grp', 'sp'), split_axis=1, concat_axis=0, tiled=True)  11.8 us
    all_to_all x1, waiting for transfers between devices, body(): lax.all_to_all(partial_value.astype(jnp.bfloat16), ('grp', 'sp'), split_a...  7.9 us
    dot_general x1, matrix products, body(): jnp.dot(group_vis, full_weight, preferred_element_type=jnp.float32)  6.62 us
    all_to_all x1, starting transfers between devices, body(): lax.all_to_all(partial_value.astype(jnp.bfloat16), ('grp', 'sp'), split_a...  4.74 us
    dot_general x1, matrix products, body(): lax.dot_general(returned, full_weight, (((1,), (1,)), ((), ())), preferre...  4.62 us
  transfers between devices with their start and end apart: 4, of which 3 were waited for; matrix products, arithmetic and copies ran while one was open for 1% of the time, Pallas kernels for 0%

commit v1 on v0

--- a/solution.py
+++ b/solution.py
@@ -10,8 +10,18 @@
     group_vis = lax.all_gather(vis, ("grp", "sp"), axis=0, tiled=True)
     full_weight = lax.all_gather(merge_weight, "dp", axis=0, tiled=True)
     partial_value = jnp.dot(group_vis, full_weight, preferred_element_type=jnp.float32)
-    emb = lax.all_to_all(
-        partial_value.astype(jnp.bfloat16), ("grp", "sp"), split_axis=0, concat_axis=1, tiled=True
+    emb = jnp.concatenate(
+        jax.lax.all_to_all(
+            jnp.stack(
+                jnp.split(
+                    partial_value.astype(jnp.bfloat16), jax.lax.psum(1, ("grp", "sp")), axis=0
+                )
+            ),
+            ("grp", "sp"),
+            0,
+            0,
+        ),
+        axis=1,
     )
     total_live = jnp.sum(img_counts)
     member = lax.axis_index("grp") * lax.axis_size("sp") + lax.axis_index("sp")

time: 230 us -> 234 us (1.017)
  local copies, waits for them, and re-layouts: 0.62 us -> 5.52 us
    unnamed x16 -> x23, local copies, waits for them, and re-layouts: 0.59 us -> 4.88 us
where the time goes in v1:
time: 234 us
  waiting for transfers between devices  143 us (61%)
  blocking collectives  51.3 us (22%)
  between operations  13.9 us (6%)
  matrix products  12.7 us (5%)
  local copies, waits for them, and re-layouts  5.52 us (2%)
  starting transfers between devices  4.72 us (2%)
  other arithmetic  2.91 us (1%)
    all_gather x1, waiting for transfers between devices, body(): full_weight = lax.all_gather(merge_weight, 'dp', axis=0, tiled=True)  106 us
    psum x1, blocking collectives, body(): gain_grad = lax.psum(part_gain, ('grp', 'dp', 'sp'))  39.5 us
    all_gather x1, waiting for transfers between devices, body(): group_vis = lax.all_gather(vis, ('grp', 'sp'), axis=0, tiled=True)  27.1 us
    all_to_all x1, blocking collectives, body(): lax.all_to_all(demb, ('grp', 'sp'), split_axis=1, concat_axis=0, tiled=True)  11.8 us
    all_to_all x1, waiting for transfers between devices, body(): jax.lax.all_to_all(jnp.stack(jnp.split(partial_value.astype(jnp.bfloat16)...  7.9 us
    dot_general x1, matrix products, body(): jnp.dot(group_vis, full_weight, preferred_element_type=jnp.float32)  5.91 us
    unnamed x23, local copies, waits for them, and re-layouts  4.88 us
  transfers between devices with their start and end apart: 4, of which 3 were waited for; matrix products, arithmetic and copies ran while one was open for 1% of the time, Pallas kernels for 0%

profile of v1, /device:TPU:0, one launch (start us, length us, event | category | flops | bytes accessed | tf_op | source)
XLA Modules:
  0.0 233.6 jit_solution(17112159985192227094)
XLA Ops:
  7.2 0.7 all-gather.3.cloned.1.call-update
  7.9 0.7 all-gather.5.cloned.1.call-update
  8.7 27.1 %all-gather.3.cloned.1.call-done = bf16[128,5120]{1,0:T(8,128)(2,1)} async-done(((bf16[16,5120]{1,0:T(8,128)(2,1)}), bf16[128,5120]{1,0:T(8,128)(2,1)}) %all-gather.3.cloned.1.call-update) | async-done | bytes 1310736 | tf_op jit(solution)/shard_map/all_gather | solution.py:10
  35.7 106.3 %all-gather.5.cloned.1.call-done = bf16[5120,1024]{1,0:T(8,128)(2,1)} async-done(((bf16[1280,1024]{1,0:T(8,128)(2,1)}), bf16[5120,1024]{1,0:T(8,128)(2,1)}) %all-gather.5.cloned.1.call-update) | async-done | bytes 10485776 | tf_op jit(solution)/shard_map/all_gather | solution.py:11
  142.1 5.9 %convolution_convert_fusion.1 = bf16[128,1024]{1,0:T(8,128)(2,1)S(1)} fusion(bf16[128,5120]{1,0:T(8,128)(2,1)} %all-gather.3.cloned.1.call-done, bf16[5120,1024]{1,0:T(8,128)(2,1)} %all-gather.5.cloned.1.call-done), kind=kOutput, calls=%fused_computation.14 | convolution fusion | flops 1342308352 | bytes 12058624 | tf_op jit(solution)/shard_map/dot_general | solution.py:12
  148.0 0.6 fusion.16
  148.6 0.6 fusion.15
  149.2 0.6 fusion.14
  149.8 0.6 fusion.13
  150.5 0.6 fusion.12
  151.1 0.6 fusion.11
  151.7 0.6 fusion.10
  152.3 0.6 fusion.9
  152.9 4.6 %all-to-all-start = ((bf16[8,16,1024]{2,1,0:T(8,128)(2,1)}), bf16[8,16,1024]{2,1,0:T(8,128)(2,1)S(1)}, u32[]{:S(2)}, u32[]{:S(2)}) async-start(bf16[8,16,1024]{2,1,0:T(8,128)(2,1)} %fusion.9), calls=%async_computation | async-start | bytes 524288 | tf_op jit(solution)/shard_map/all_to_all | solution.py:14
  157.6 0.6 reduce_sum.36
  158.2 0.7 add_compare_fusion
  159.0 7.9 %all-to-all-done = bf16[8,16,1024]{2,1,0:T(8,128)(2,1)S(1)} async-done(((bf16[8,16,1024]{2,1,0:T(8,128)(2,1)}), bf16[8,16,1024]{2,1,0:T(8,128)(2,1)S(1)}, u32[]{:S(2)}, u32[]{:S(2)}) %all-to-all-start) | async-done | bytes 262176 | tf_op jit(solution)/shard_map/all_to_all | solution.py:14
  166.9 1.0 multiply_reduce_fusion
  167.9 0.6 copy-done.1
  168.5 1.5 fusion.7
  170.0 1.1 fusion
  171.2 11.8 %all_to_all.24 = bf16[16,8,1024]{2,0,1:T(8,128)(2,1)S(1)} all-to-all(bf16[16,8,1024]{2,0,1:T(8,128)(2,1)S(1)} %bitcast.52), channel_id=1, replica_groups=mesh['grp'=2,'dp'=4,'sp'=4] {'grp','sp'}, dimensions={1} | all-to-all | bytes 524288 | tf_op jit(solution)/shard_map/all_to_all | solution.py:44
  183.0 4.6 %convolution_convert_fusion = bf16[128,5120]{1,0:T(8,128)(2,1)} fusion(bf16[128,1024]{1,0:T(8,128)(2,1)S(1)} %bitcast.50, bf16[5120,1024]{1,0:T(8,128)(2,1)S(1)} %bitcast.48), kind=kOutput, calls=%fused_computation.3 | convolution fusion | flops 1342832640 | bytes 12058624 | tf_op jit(solution)/shard_map/dot_general | solution.py:45
  187.6 39.5 %psum.7 = f32[8192]{0:T(1024)} all-reduce(f32[8192]{0:T(1024)S(1)} %get-tuple-element.2), channel_id=1, replica_groups=mesh['grp'=2,'dp'=4,'sp'=4] {'grp','dp','sp'}, use_global_device_ids=true, to_apply=%region_6.7 | all-reduce | flops 8192 | bytes 65536 | tf_op jit(solution)/shard_map/psum | solution.py:51
  (26 shorter events, 0.3 us)
Async XLA Ops:
  7.2 28.6 %all-gather.3.cloned.1.call-start = ((), (), s32[]{:S(2)}) async-start(), calls=%async_computation.3 | async-start | bytes 1474560 | tf_op jit(solution)/shard_map/all_gather | solution.py:10
  7.9 134.2 %all-gather.5.cloned.1.call-start = ((), (), s32[]{:S(2)}) async-start(), calls=%async_computation.4 | async-start | bytes 13107200 | tf_op jit(solution)/shard_map/all_gather | solution.py:11
  8.6 148.9 %copy-start.4 = (s32[8]{0:T(128)S(1)}, s32[8]{0:T(128)}, u32[]{:S(2)}) copy-start(s32[8]{0:T(128)} %param.9) | copy-start | bytes 100
  8.7 150.2 %copy-start.3 = (s32[16]{0:T(128)S(1)}, s32[16]{0:T(128)}, u32[]{:S(2)}) copy-start(s32[16]{0:T(128)} %param.10) | copy-start | bytes 196
  8.7 158.2 %copy-start = (bf16[128,8192]{1,0:T(8,128)(2,1)S(1)}, bf16[128,8192]{1,0:T(8,128)(2,1)}, u32[]{:S(2)}) copy-start(bf16[128,8192]{1,0:T(8,128)(2,1)} %param.11) | copy-start | bytes 6291460
  148.0 19.9 %copy-start.2 = (f32[8192]{0:T(1024)S(1)}, f32[8192]{0:T(1024)}, u32[]{:S(2)}) copy-start(f32[8192]{0:T(1024)} %param.13) | copy-start | bytes 98308
  152.9 14.0 %all-to-all-start = ((bf16[8,16,1024]{2,1,0:T(8,128)(2,1)}), bf16[8,16,1024]{2,1,0:T(8,128)(2,1)S(1)}, u32[]{:S(2)}, u32[]{:S(2)}) async-start(bf16[8,16,1024]{2,1,0:T(8,128)(2,1)} %fusion.9), calls=%async_computation | async-start | bytes 524288 | tf_op jit(solution)/shard_map/all_to_all | solution.py:14
  157.5 69.6 %reduce-scatter.2.cloned.1.call-start = ((), (), s32[]{:S(2)}) async-start(), calls=%async_computation.5 | async-start | bytes 1474560 | tf_op jit(solution)/shard_map/reduce_scatter | solution.py:48
  166.9 1.6 copy-start.1
  166.9 16.0 %slice-start = ((s8[10485760]{0:T(1024)(128)(4,1)}), s8[4194304]{0:T(1024)(128)(4,1)S(1)}, s32[]{:S(2)}) async-start(s8[10485760]{0:T(1024)(128)(4,1)} %bitcast.47), calls=%async_computation.6 | async-start | bytes 8388608
  168.5 14.5 %slice-start.1 = ((s8[10485760]{0:T(1024)(128)(4,1)}), s8[4194304]{0:T(1024)(128)(4,1)S(1)}, s32[]{:S(2)}) async-start(s8[10485760]{0:T(1024)(128)(4,1)} %bitcast.47), calls=%async_computation.7 | async-start | bytes 8388608
  170.0 13.0 %slice-start.2 = ((s8[10485760]{0:T(1024)(128)(4,1)}), s8[2097152]{0:T(1024)(128)(4,1)S(1)}, s32[]{:S(2)}) async-start(s8[10485760]{0:T(1024)(128)(4,1)} %bitcast.47), calls=%async_computation.8 | async-start | bytes 4194304
Sparse Core Ops, SparseCore 0:
  9.6 26.1 all-gather.2
  37.6 104.4 all-gather.4
  187.7 35.0 reduce-scatter.1
